TPU v7x, 512 devices: a whole 4x4x16 slice. The times are simulated.
512 devices in a mesh: dp: 4 (over x), ep: 128 (over y, z, core).
Axes of the slice: x: 4, y: 4, z: 16, core: 2. Of those that a mesh axis runs over, the one named last changes fastest.
Arguments:
- hidden_states: bfloat16 [4096, 3584], P(('dp', 'ep')), parts along dimension 0, may hold values from -120 to 120
- norm_gain: float32 [3584], replicated, may hold values from 0.1 to 1.9
- expert_ids: int32 [4096, 8], P(('dp', 'ep')), parts along dimension 0, may hold values from 0 to 15, all different within a row; in each aligned block of 8 rows (0 to 7, 8 to 15, ...) at most 5 rows name the same one
- route_scores: float32 [4096, 8], P(('dp', 'ep')), parts along dimension 0, may hold values from 0.1 to 1
- gate_weight: bfloat16 [3584, 16384], P(None, 'ep'), may hold values from -0.09375 to 0.09375
- up_weight: bfloat16 [3584, 16384], P(None, 'ep'), may hold values from -0.09375 to 0.09375
- down_weight: bfloat16 [16384, 3584], P('ep'), may hold values from -0.1875 to 0.1875
- query_latent: bfloat16 [4096, 64, 512], P(('dp', 'ep')), parts along dimension 0, may hold values from -23 to 23
- query_rope: bfloat16 [4096, 4096], P(('dp', 'ep')), parts along dimension 0, may hold values from -23 to 23
- cache_latent: bfloat16 [512, 512, 512], P(('dp', 'ep')), parts along dimension 0, may hold values from -5.3 to 5.3
- cache_rope: bfloat16 [512, 64, 512], P(('dp', 'ep')), parts along dimension 0, may hold values from -5.3 to 5.3
- tree_latent: bfloat16 [4096, 512], P(('dp', 'ep')), parts along dimension 0, may hold values from -6 to 6
- tree_rope: bfloat16 [4096, 64], P(('dp', 'ep')), parts along dimension 0, may hold values from -6 to 6
- cache_lengths: int32 [512], P(('dp', 'ep')), parts along dimension 0, may hold values from 128 to 512, as said below
- tree_parents: int32 [4096], P(('dp', 'ep')), parts along dimension 0, may hold values from 0 to 6, as said below
Outputs:
- attention_out: bfloat16 [4096, 64, 512], P(('dp', 'ep')), parts along dimension 0
- expert_out: bfloat16 [4096, 3584], P(('dp', 'ep')), parts along dimension 0
There are 4 independent parts, one for each index of `dp`. A program takes and returns all parts, laid end to end along the dimension named above; an argument that names none is the same for every part. Nothing has to cross between parts.
Inputs may be any that keep to these rules, and one draw needn't show every extreme that they name: `expert_ids`: in the 8 rows of one device each expert is named by at most 5 rows, a bound that some block reaches; each row names 8 different experts. `cache_lengths`: some request holds exactly 512 positions. `tree_parents`: counting candidates from 0 within their request, candidate i > 0 has a parent below i, and candidate 0 has 0.
All inputs are finite; a program needn't handle non-finite values.
Results may differ from a plain program's by a relative error of at most 0.008.
Values may be sent and summed in bfloat16 or wider, within the bound.
No kernel may reach another device: no remote copies, remote signals or barrier semaphores. Data moves between devices by JAX's collectives and lax.ppermute only.
A program may use at most 64 MiB of HBM per device.

v0:
```python
import jax
import jax.numpy as jnp
from jax import lax
from jax.sharding import Mesh, PartitionSpec as P

HID = 1024
EXPERTS = 16
softmax_scale = 192.0 ** (-0.5)
route_scale = 2.5
norm_eps = 1e-06
very_negative = -1e30
grid_axes = ("dp", "y", "z", "c")


def visible_tree(parents):
    tree_size = parents.shape[0]
    position = jnp.arange(tree_size, dtype=jnp.int32)
    parent_map = ((parents[:, None] == position[None, :]) & (position[:, None] > 0)).astype(
        jnp.float32
    )
    identity = jnp.eye(tree_size, dtype=jnp.float32)
    reached = identity
    for sweep_index in range(tree_size):
        reached = jnp.minimum(
            identity + jnp.dot(parent_map, reached, precision=lax.Precision.HIGHEST), 1.0
        )
    return reached > 0.5


def attend_request(
    query_latent,
    query_rope,
    cache_latent,
    cache_rope,
    tree_latent,
    tree_rope,
    cache_length,
    parents,
):
    row_count = query_latent.shape[0]
    head_count = query_latent.shape[1]
    rope_width = tree_rope.shape[1]
    query_rotary = query_rope.reshape(row_count, head_count, rope_width)
    cache_scores = jnp.einsum(
        "rhc,lc->rhl", query_latent, cache_latent, preferred_element_type=jnp.float32
    )
    cache_scores = (
        cache_scores
        + jnp.einsum("rhc,cl->rhl", query_rotary, cache_rope, preferred_element_type=jnp.float32)
    ) * softmax_scale
    candidate_tree_scores = jnp.einsum(
        "rhc,jc->rhj", query_latent, tree_latent, preferred_element_type=jnp.float32
    )
    candidate_tree_scores = (
        candidate_tree_scores
        + jnp.einsum("rhc,jc->rhj", query_rotary, tree_rope, preferred_element_type=jnp.float32)
    ) * softmax_scale
    cache_live = (jnp.arange(cache_latent.shape[0], dtype=jnp.int32) < cache_length)[None, None, :]
    tree_seen = visible_tree(parents)[:, None, :]
    cache_scores = jnp.where(cache_live, cache_scores, very_negative)
    candidate_tree_scores = jnp.where(tree_seen, candidate_tree_scores, very_negative)
    row_peak = jnp.maximum(
        jnp.max(cache_scores, axis=-1, keepdims=True),
        jnp.max(candidate_tree_scores, axis=-1, keepdims=True),
    )
    cache_exp = jnp.where(cache_live, jnp.exp(cache_scores - row_peak), 0.0)
    tree_exp = jnp.where(tree_seen, jnp.exp(candidate_tree_scores - row_peak), 0.0)
    denominator = jnp.sum(cache_exp, axis=-1, keepdims=True) + jnp.sum(
        tree_exp, axis=-1, keepdims=True
    )
    cache_probs = (cache_exp / denominator).astype(jnp.bfloat16)
    tree_probs = (tree_exp / denominator).astype(jnp.bfloat16)
    attended = jnp.einsum(
        "rhl,lc->rhc", cache_probs, cache_latent, preferred_element_type=jnp.float32
    )
    attended = attended + jnp.einsum(
        "rhj,jc->rhc", tree_probs, tree_latent, preferred_element_type=jnp.float32
    )
    return attended.astype(jnp.bfloat16)


def combine_table(expert_ids, route_scores):
    router_weight_matrix = (
        route_scale * route_scores / jnp.sum(route_scores, axis=-1, keepdims=True)
    ).astype(jnp.bfloat16)
    matches = expert_ids[:, :, None] == jnp.arange(EXPERTS, dtype=jnp.int32)[None, None, :]
    return jnp.sum(
        jnp.where(matches, router_weight_matrix.astype(jnp.float32)[:, :, None], 0.0), axis=1
    ).astype(jnp.bfloat16)


def swap_core(value):
    return lax.ppermute(value, "c", [(0, 1), (1, 0)])


def gated(rows, share, gate_weight, up_weight, down_weight):
    gate_act = jnp.dot(rows, gate_weight, preferred_element_type=jnp.float32)
    up_act = jnp.dot(rows, up_weight, preferred_element_type=jnp.float32)
    hidden = (share * jax.nn.silu(gate_act) * up_act).astype(jnp.bfloat16)
    return jnp.dot(hidden, down_weight, preferred_element_type=jnp.float32)


def local(
    hidden_states,
    norm_gain,
    expert_ids,
    route_scores,
    gate_weight,
    up_weight,
    down_weight,
    query_latent,
    query_rope,
    cache_latent,
    cache_rope,
    tree_latent,
    tree_rope,
    cache_lengths,
    tree_parents,
):
    other = [swap_core(w) for w in (gate_weight, up_weight, down_weight)]
    states = hidden_states.astype(jnp.float32)
    normed = (
        states * lax.rsqrt(jnp.mean(states * states, axis=-1, keepdims=True) + norm_eps) * norm_gain
    ).astype(jnp.bfloat16)
    width = normed.shape[1]
    combine = combine_table(expert_ids, route_scores)
    packed = jnp.concatenate([normed, jnp.pad(combine, ((0, 0), (0, 128 - EXPERTS)))], axis=1)
    gathered = lax.all_gather(packed, ("y", "z"), axis=0, tiled=True)
    attention_out = attend_request(
        query_latent,
        query_rope,
        cache_latent[0],
        cache_rope[0],
        tree_latent,
        tree_rope,
        cache_lengths[0],
        tree_parents,
    )
    chip = lax.axis_index("y") * lax.axis_size("z") + lax.axis_index("z")
    unit_count = 2 * gate_weight.shape[1]
    expert = chip * unit_count // HID
    rows = gathered[:, :width]
    shares = gathered[:, width:].astype(jnp.float32)
    share = jnp.sum(
        jnp.where(jnp.arange(shares.shape[1])[None, :] == expert, shares, 0.0),
        axis=1,
        keepdims=True,
    )
    partial = gated(rows, share, gate_weight, up_weight, down_weight) + gated(rows, share, *other)
    expert_out = lax.psum_scatter(
        partial.astype(jnp.bfloat16), ("y", "z"), scatter_dimension=0, tiled=True
    )
    return (attention_out, expert_out)


def solution(mesh):
    devices = mesh.devices.reshape(4, 4, 16, 2)
    grid = Mesh(devices, grid_axes)
    rows = P(grid_axes, None)
    ep = ("y", "z", "c")
    placed = (
        rows,
        P(),
        rows,
        rows,
        P(None, ep),
        P(None, ep),
        P(ep, None),
        P(grid_axes, None, None),
        rows,
        P(grid_axes, None, None),
        P(grid_axes, None, None),
        rows,
        rows,
        P(grid_axes),
        P(grid_axes),
    )
    return jax.shard_map(
        local,
        mesh=grid,
        in_specs=placed,
        out_specs=(P(grid_axes, None, None), rows),
        check_vma=False,
    )
```

profile of v0, /device:TPU:2, one launch (start us, length us, event | category | flops | bytes accessed | tf_op | source)
XLA Modules:
  0.0 896.7 jit_solution(6409630612788064503)
XLA Ops:
  7.2 0.0 copy-start
  7.2 0.0 all-gather.2.cloned.1.call-start
  7.2 1.0 fusion.54
  8.2 0.8 reduce_sum.57
  9.1 0.8 fusion.76
  9.8 0.9 fusion.56
  10.7 0.8 select_reduce_fusion.1
  11.5 0.6 fusion.58
  12.1 0.0 all-gather.2.cloned.1.call-update
  12.2 0.0 reduce-scatter.2.cloned.1.call-start
  12.2 1.9 collective-permute-start.1
  14.1 2.4 collective-permute-start
  16.6 1.9 collective-permute-start.2
  18.5 143.6 %all-gather.2.cloned.1.call-done = bf16[512,3712]{1,0:T(8,128)(2,1)} async-done(((bf16[8,3712]{1,0:T(8,128)(2,1)}), bf16[512,3712]{1,0:T(8,128)(2,1)}) %all-gather.2.cloned.1.call-update) | async-done | bytes 3801104 | tf_op jit(solution)/shard_map/all_gather | solution.py:128
  162.1 0.0 copy-start.1
  162.1 1.2 select_reduce_fusion
  163.2 4.1 fusion.6
  167.4 0.0 copy-start.3
  167.4 0.0 copy-start.4
  167.4 0.0 collective-permute-done.1
  167.4 0.0 copy-done.1
  167.4 2.4 fusion
  169.8 0.0 copy-done.3
  169.8 0.0 copy-done.4
  169.9 9.0 fusion.18
  178.8 0.0 copy-start.5
  178.8 0.0 collective-permute-done
  178.8 0.0 collective-permute-done.2
  178.8 10.4 %add_convert_fusion = bf16[512,3584]{1,0:T(8,128)(2,1)} fusion(f32[512,3584]{1,0:T(8,128)} %fusion.18, bf16[128,3584]{1,0:T(8,128)(2,1)} %collective-permute-done.2, f32[512,128]{1,0:T(8,128)S(1)} %fusion, bf16[3584,128]{1,0:T(8,128)(2,1)S(1)} %collective-permute-done, bf16[512,3712]{1,0:T(8,128)(2,1)} %all-gather.2.cloned.1.call-done, ...), kind=kOutput, calls=%fused_computation | convolution fusion | flops 943652864 | bytes 16779264 | tf_op jit(solution)/shard_map/dot_general | solution.py:100
  189.2 0.0 copy-start.9
  189.2 0.0 copy-start.2
  189.2 0.0 copy-start.7
  189.2 0.0 copy-start.8
  189.2 0.0 copy-start.6
  189.2 0.0 reduce-scatter.2.cloned.1.call-update
  189.2 0.0 copy-done.5
  189.2 0.2 reshape.48
  190.1 0.0 copy-done.9
  190.1 0.2 fusion.29
  190.3 0.2 fusion.28
  190.5 0.2 fusion.27
  190.7 0.2 fusion.26
  190.9 0.2 fusion.25
  191.1 0.2 fusion.24
  191.3 0.2 fusion.23
  191.5 0.2 fusion.30
  191.7 0.0 copy-done.2
  191.7 0.0 copy-done.7
  191.7 0.3 fusion.65
  192.0 0.0 copy-done.8
  192.0 0.2 fusion.99
  192.3 0.0 copy-done
  192.3 0.5 fusion.34
  192.8 0.0 copy-done.6
  192.8 0.4 fusion.98
  193.1 0.1 fusion.59
  193.2 0.3 fusion.31
  193.6 0.5 fusion.32
  194.1 1.2 fusion.10
  195.4 694.5 %reduce-scatter.2.cloned.1.call-done = bf16[8,3584]{1,0:T(8,128)(2,1)} async-done(((bf16[512,3584]{1,0:T(8,128)(2,1)}), bf16[8,3584]{1,0:T(8,128)(2,1)}) %reduce-scatter.2.cloned.1.call-update) | async-done | bytes 57360 | tf_op jit(solution)/shard_map/reduce_scatter | solution.py:150
  (6 shorter events, 0.0 us)
Async XLA Ops:
  7.2 185.1 %copy-start = (bf16[1,512,512]{2,1,0:T(8,128)(2,1)S(1)}, bf16[1,512,512]{2,1,0:T(8,128)(2,1)}, u32[]{:S(2)}) copy-start(bf16[1,512,512]{2,1,0:T(8,128)(2,1)} %param.24) | copy-start | bytes 1572868
  7.2 154.9 %all-gather.2.cloned.1.call-start = ((), (), s32[]{:S(2)}) async-start(), calls=%async_computation.1 | async-start | bytes 3860480 | tf_op jit(solution)/shard_map/all_gather | solution.py:128
  12.2 877.7 %reduce-scatter.2.cloned.1.call-start = ((), (), s32[]{:S(2)}) async-start(), calls=%async_computation.2 | async-start | bytes 3727360 | tf_op jit(solution)/shard_map/reduce_scatter | solution.py:150
  12.2 155.2 %collective-permute-start.1 = (bf16[3584,128]{1,0:T(8,128)(2,1)}, bf16[3584,128]{1,0:T(8,128)(2,1)}, u32[]{:S(2)}, u32[]{:S(2)}) collective-permute-start(bf16[3584,128]{1,0:T(8,128)(2,1)} %param.20), channel_id=1, source_target_pairs={{0,1},{1,0},{2,3},{3,2},{4,5},{5,4},{6,7},{7,6},{8,9},{9,8},{10,11... | collective-permute-start | bytes 2752520 | tf_op jit(solution)/shard_map/ppermute | solution.py:93
  14.1 164.7 %collective-permute-start = (bf16[3584,128]{1,0:T(8,128)(2,1)}, bf16[3584,128]{1,0:T(8,128)(2,1)S(1)}, u32[]{:S(2)}, u32[]{:S(2)}) collective-permute-start(bf16[3584,128]{1,0:T(8,128)(2,1)} %param.19), channel_id=1, source_target_pairs={{0,1},{1,0},{2,3},{3,2},{4,5},{5,4},{6,7},{7,6},{8,9},{9,8},{10,11... | collective-permute-start | bytes 2752520 | tf_op jit(solution)/shard_map/ppermute | solution.py:93
  16.6 162.3 %collective-permute-start.2 = (bf16[128,3584]{1,0:T(8,128)(2,1)}, bf16[128,3584]{1,0:T(8,128)(2,1)}, u32[]{:S(2)}, u32[]{:S(2)}) collective-permute-start(bf16[128,3584]{1,0:T(8,128)(2,1)} %param.21), channel_id=1, source_target_pairs={{0,1},{1,0},{2,3},{3,2},{4,5},{5,4},{6,7},{7,6},{8,9},{9,8},{10,11... | collective-permute-start | bytes 2752520 | tf_op jit(solution)/shard_map/ppermute | solution.py:93
  162.1 5.3 copy-start.1
  167.4 2.4 copy-start.3
  167.4 2.5 copy-start.4
  178.8 10.4 %copy-start.5 = (bf16[8,4096]{1,0:T(8,128)(2,1)S(1)}, bf16[8,4096]{1,0:T(8,128)(2,1)}, u32[]{:S(2)}) copy-start(bf16[8,4096]{1,0:T(8,128)(2,1)} %param.23) | copy-start | bytes 196612
  189.2 1.0 copy-start.9
  189.2 2.5 copy-start.2
  189.2 2.5 copy-start.7
  189.2 2.9 copy-start.8
  189.2 3.6 copy-start.6
Sparse Core Ops, SparseCore 0:
  12.3 149.7 all-gather.1
  189.3 700.4 reduce-scatter.1
where the time goes:
time: 897 us
  waiting for transfers between devices  838 us (93%)
  matrix products  30.5 us (3%)
  between operations  15 us (2%)
    reduce_scatter x1, waiting for transfers between devices, local(): lax.psum_scatter(partial.astype(jnp.bfloat16), ('y', 'z'), scatter_dimens...  695 us
    all_gather x1, waiting for transfers between devices, local(): gathered = lax.all_gather(packed, ('y', 'z'), axis=0, tiled=True)  144 us
    dot_general x2, matrix products, gated(): return jnp.dot(hidden, down_weight, preferred_element_type=jnp.float32)  19.3 us
  transfers between devices with their start and end apart: 5, of which 2 were waited for; matrix products, arithmetic and copies ran while one was open for 2% of the time, Pallas kernels for 0%

commit v1 on v0

--- a/solution.py
+++ b/solution.py
@@ -125,7 +125,9 @@
     width = normed.shape[1]
     combine = combine_table(expert_ids, route_scores)
     packed = jnp.concatenate([normed, jnp.pad(combine, ((0, 0), (0, 128 - EXPERTS)))], axis=1)
-    gathered = lax.all_gather(packed, ("y", "z"), axis=0, tiled=True)
+    gathered = jnp.concatenate(
+        lax.all_to_all(jnp.stack([packed] * lax.axis_size(("y", "z"))), ("y", "z"), 0, 0), axis=0
+    )
     attention_out = attend_request(
         query_latent,
         query_rope,

time: 897 us -> 938 us (1.046)
  the two profiles are of different devices: /device:TPU:2 before, /device:TPU:6 now
where the time goes in v1:
time: 938 us
  waiting for transfers between devices  858 us (91%)
  matrix products  31.5 us (3%)
  starting transfers between devices  25.4 us (3%)
  between operations  15 us (2%)
    reduce_scatter x1, waiting for transfers between devices, local(): lax.psum_scatter(partial.astype(jnp.bfloat16), ('y', 'z'), scatter_dimens...  693 us
    all_to_all x1, waiting for transfers between devices, local(): lax.all_to_all(jnp.stack([packed] * lax.axis_size(('y', 'z'))), ('y', 'z'...  165 us
    dot_general x2, matrix products, gated(): return jnp.dot(hidden, down_weight, preferred_element_type=jnp.float32)  19.3 us
    all_to_all x1, starting transfers between devices, local(): lax.all_to_all(jnp.stack([packed] * lax.axis_size(('y', 'z'))), ('y', 'z'...  19.1 us
  transfers between devices with their start and end apart: 5, of which 2 were waited for; matrix products, arithmetic and copies ran while one was open for 2% of the time, Pallas kernels for 0%

profile of v1, /device:TPU:6, one launch (start us, length us, event | category | flops | bytes accessed | tf_op | source)
XLA Modules:
  0.0 938.0 jit_solution(15049975402484868074)
XLA Ops:
  7.2 0.0 copy-start
  7.2 1.0 fusion.54
  8.2 0.8 reduce_sum.57
  9.0 0.8 fusion.76
  9.8 0.9 fusion.56
  10.7 0.8 select_reduce_fusion.1
  11.5 2.1 stack.2
  13.6 0.0 copy-start.2
  13.6 0.0 copy-start.3
  13.6 19.1 %all-to-all-start = ((bf16[64,8,3712]{2,1,0:T(8,128)(2,1)}), bf16[64,8,3712]{2,1,0:T(8,128)(2,1)}, u32[]{:S(2)}, u32[]{:S(2)}) async-start(bf16[64,8,3712]{2,1,0:T(8,128)(2,1)} %stack.2), calls=%async_computation | async-start | bytes 7602176 | tf_op jit(solution)/shard_map/all_to_all | solution.py:129
  32.7 0.0 reduce-scatter.2.cloned.1.call-start
  32.7 0.0 copy-done.2
  32.7 1.9 collective-permute-start.1
  34.7 2.4 collective-permute-start
  37.1 0.0 copy-done.3
  37.1 1.9 collective-permute-start.2
  39.0 164.9 %all-to-all-done = bf16[64,8,3712]{2,1,0:T(8,128)(2,1)} async-done(((bf16[64,8,3712]{2,1,0:T(8,128)(2,1)}), bf16[64,8,3712]{2,1,0:T(8,128)(2,1)}, u32[]{:S(2)}, u32[]{:S(2)}) %all-to-all-start) | async-done | bytes 3801120 | tf_op jit(solution)/shard_map/all_to_all | solution.py:129
  203.9 1.0 select_reduce_fusion
  204.9 4.1 fusion.6
  209.0 0.0 collective-permute-done.1
  209.0 3.4 fusion
  212.4 9.0 fusion.18
  221.4 0.0 copy-start.4
  221.4 0.0 collective-permute-done
  221.4 0.0 collective-permute-done.2
  221.4 10.4 %add_convert_fusion = bf16[512,3584]{1,0:T(8,128)(2,1)} fusion(f32[512,3584]{1,0:T(8,128)} %fusion.18, bf16[128,3584]{1,0:T(8,128)(2,1)} %collective-permute-done.2, f32[512,128]{1,0:T(8,128)S(1)} %fusion, bf16[3584,128]{1,0:T(8,128)(2,1)S(1)} %collective-permute-done, bf16[512,3712]{1,0:T(8,128)(2,1)} %bitcast.7, f32[512]{0:T(512)S(1)} %select_reduce_fusion), kind=kOutput, calls=%fused_computation | convolution fusion | flops 943652864 | bytes 16779264 | tf_op jit(solution)/shard_map/dot_general | solution.py:100
  231.8 0.0 copy-start.8
  231.8 0.0 copy-start.1
  231.8 0.0 copy-start.6
  231.8 0.0 copy-start.7
  231.8 0.0 copy-start.5
  231.8 0.0 reduce-scatter.2.cloned.1.call-update
  231.8 0.0 copy-done.4
  231.8 0.2 reshape.53
  232.7 0.0 copy-done.8
  232.7 0.2 fusion.29
  232.9 0.2 fusion.28
  233.1 0.2 fusion.27
  233.3 0.2 fusion.26
  233.5 0.2 fusion.25
  233.7 0.2 fusion.24
  233.9 0.2 fusion.23
  234.1 0.2 fusion.30
  234.3 0.0 copy-done.1
  234.3 0.0 copy-done.6
  234.3 0.3 fusion.65
  234.6 0.0 copy-done.7
  234.6 0.2 fusion.99
  234.9 0.0 copy-done
  234.9 0.5 fusion.34
  235.4 0.0 copy-done.5
  235.4 0.4 fusion.98
  235.7 0.1 fusion.59
  235.8 0.4 fusion.31
  236.2 0.5 fusion.32
  236.7 1.2 fusion.10
  238.0 693.2 %reduce-scatter.2.cloned.1.call-done = bf16[8,3584]{1,0:T(8,128)(2,1)} async-done(((bf16[512,3584]{1,0:T(8,128)(2,1)}), bf16[8,3584]{1,0:T(8,128)(2,1)}) %reduce-scatter.2.cloned.1.call-update) | async-done | bytes 57360 | tf_op jit(solution)/shard_map/reduce_scatter | solution.py:152
  (7 shorter events, 0.0 us)
Async XLA Ops:
  7.2 227.7 %copy-start = (bf16[1,512,512]{2,1,0:T(8,128)(2,1)S(1)}, bf16[1,512,512]{2,1,0:T(8,128)(2,1)}, u32[]{:S(2)}) copy-start(bf16[1,512,512]{2,1,0:T(8,128)(2,1)} %param.24) | copy-start | bytes 1572868
  13.6 19.2 %copy-start.2 = (bf16[3584,128]{1,0:T(8,128)(2,1)S(1)}, bf16[3584,128]{1,0:T(8,128)(2,1)}, u32[]{:S(2)}) copy-start(bf16[3584,128]{1,0:T(8,128)(2,1)} %param.20) | copy-start | bytes 2752516
  13.6 23.5 %copy-start.3 = (bf16[128,3584]{1,0:T(8,128)(2,1)S(1)}, bf16[128,3584]{1,0:T(8,128)(2,1)}, u32[]{:S(2)}) copy-start(bf16[128,3584]{1,0:T(8,128)(2,1)} %param.21) | copy-start | bytes 2752516
  13.6 190.3 %all-to-all-start = ((bf16[64,8,3712]{2,1,0:T(8,128)(2,1)}), bf16[64,8,3712]{2,1,0:T(8,128)(2,1)}, u32[]{:S(2)}, u32[]{:S(2)}) async-start(bf16[64,8,3712]{2,1,0:T(8,128)(2,1)} %stack.2), calls=%async_computation | async-start | bytes 7602176 | tf_op jit(solution)/shard_map/all_to_all | solution.py:129
  32.7 898.5 %reduce-scatter.2.cloned.1.call-start = ((), (), s32[]{:S(2)}) async-start(), calls=%async_computation.2 | async-start | bytes 3727360 | tf_op jit(solution)/shard_map/reduce_scatter | solution.py:152
  32.7 176.3 %collective-permute-start.1 = (bf16[3584,128]{1,0:T(8,128)(2,1)S(1)}, bf16[3584,128]{1,0:T(8,128)(2,1)}, u32[]{:S(2)}, u32[]{:S(2)}) collective-permute-start(bf16[3584,128]{1,0:T(8,128)(2,1)S(1)} %copy-done.2), channel_id=1, source_target_pairs={{0,1},{1,0},{2,3},{3,2},{4,5},{5,4},{6,7},{7,6},{8,9},{9,8},{10,11... | collective-permute-start | bytes 2752520 | tf_op jit(solution)/shard_map/ppermute | solution.py:93
  34.7 186.7 %collective-permute-start = (bf16[3584,128]{1,0:T(8,128)(2,1)}, bf16[3584,128]{1,0:T(8,128)(2,1)S(1)}, u32[]{:S(2)}, u32[]{:S(2)}) collective-permute-start(bf16[3584,128]{1,0:T(8,128)(2,1)} %param.19), channel_id=1, source_target_pairs={{0,1},{1,0},{2,3},{3,2},{4,5},{5,4},{6,7},{7,6},{8,9},{9,8},{10,11... | collective-permute-start | bytes 2752520 | tf_op jit(solution)/shard_map/ppermute | solution.py:93
  37.1 184.3 %collective-permute-start.2 = (bf16[128,3584]{1,0:T(8,128)(2,1)S(1)}, bf16[128,3584]{1,0:T(8,128)(2,1)}, u32[]{:S(2)}, u32[]{:S(2)}) collective-permute-start(bf16[128,3584]{1,0:T(8,128)(2,1)S(1)} %copy-done.3), channel_id=1, source_target_pairs={{0,1},{1,0},{2,3},{3,2},{4,5},{5,4},{6,7},{7,6},{8,9},{9,8},{10,11... | collective-permute-start | bytes 2752520 | tf_op jit(solution)/shard_map/ppermute | solution.py:93
  221.4 10.4 %copy-start.4 = (bf16[8,4096]{1,0:T(8,128)(2,1)S(1)}, bf16[8,4096]{1,0:T(8,128)(2,1)}, u32[]{:S(2)}) copy-start(bf16[8,4096]{1,0:T(8,128)(2,1)} %param.23) | copy-start | bytes 196612
  231.8 1.0 copy-start.8
  231.8 2.5 copy-start.1
  231.8 2.5 copy-start.6
  231.8 2.9 copy-start.7
  231.8 3.6 copy-start.5
Sparse Core Ops, SparseCore 0:
  231.9 699.1 reduce-scatter.1
